TPU v7x, 32 devices: a whole 2x2x4 slice. The times are simulated.
32 devices in a mesh: scan: 8 (over z, x), tile: 4 (over y, core).
Axes of the slice: x: 2, y: 2, z: 4, core: 2. Of those that a mesh axis runs over, the one named last changes fastest.
Arguments:
- object_slab: float32 [2, 3072, 6144], P(None, 'tile', 'scan'), may hold values from -6 to 6
- probe_field: float32 [2, 512, 512], replicated, may hold values from -3 to 3
- intensities: bfloat16 [8, 4, 6, 512, 512], P('scan', 'tile'), may hold values from 0 to 2
- offsets: int32 [8, 4, 6, 2], P('scan', 'tile'), may hold values from 0 to 767
- live_count: int32 [8, 4], P(None, 'tile'), may hold values from 1 to 6, as said below
Outputs:
- object_grad: float32 [2, 3072, 6144], P(None, 'tile', 'scan')
Inputs may be any that keep to these rules, and one draw needn't show every extreme that they name: The first live_count slots of a group hold its measured positions; some group has all 6 slots live.
All inputs are finite; a program needn't handle non-finite values.
Results may differ from a plain program's by a relative error of at most 0.014.
Values may be sent and summed in bfloat16 or wider, within the bound.
A program may use at most 128 MiB of HBM per device.

v0:
```python
import functools
import math

import jax
import jax.numpy as jnp
import numpy as np
from jax import lax
from jax.experimental import pallas as pl
from jax.experimental.pallas import tpu as pltpu
from jax.sharding import PartitionSpec as P

RADIX = 4
LANES = 128


def residue_tables(side_len):
    part = side_len // RADIX
    freq = np.arange(side_len).reshape(part, RADIX).T
    across = np.arange(part)
    phase = (freq[:, :, None] * across[None, None, :] % side_len) * (2.0 * math.pi / side_len)
    factor = 1.0 / math.sqrt(side_len)
    cos = np.cos(phase) * factor
    sin = np.sin(phase) * factor
    rows = np.concatenate(
        [np.concatenate([cos, sin], axis=2), np.concatenate([-sin, cos], axis=2)], axis=1
    ).astype(np.float32)
    return jnp.asarray(rows, jnp.bfloat16), jnp.asarray(rows.swapaxes(1, 2), jnp.bfloat16)


def sorted_by_residue(side_len):
    at = np.arange(side_len)
    source = at % (side_len // RADIX) * RADIX + at // (side_len // RADIX)
    sort = (source[:, None] == at[None, :]).astype(np.float32)
    return jnp.asarray(sort, jnp.bfloat16), jnp.asarray(sort.T, jnp.bfloat16)


def dot(a, b):
    return jnp.dot(a, b, preferred_element_type=jnp.float32)


def butterfly(parts, sign):
    (r0, i0), (r1, i1), (r2, i2), (r3, i3) = parts
    ar, ai, br, bi = r0 + r2, i0 + i2, r1 + r3, i1 + i3
    cr, ci, dr, di = r0 - r2, i0 - i2, r1 - r3, i1 - i3
    plus = (cr - di, ci + dr)
    minus = (cr + di, ci - dr)
    first, third = (plus, minus) if sign > 0 else (minus, plus)
    return [(ar + br, ai + bi), first, (ar - br, ai - bi), third]


def neighbours(axes):
    result = []
    for name, count in axes:
        me = lax.axis_index(name)
        result.append((me > 0, {name: me - 1}, me < count - 1, {name: me + 1}))
    return result


def meet(peers):
    barrier = pltpu.get_barrier_semaphore()
    for has_low, low, has_high, high in peers:
        for there, peer in ((has_low, low), (has_high, high)):

            @pl.when(there)
            def _(peer=peer):
                pl.semaphore_signal(
                    barrier, inc=1, device_id=peer, device_id_type=pl.DeviceIdType.MESH
                )

    count = sum(
        there.astype(jnp.int32) for has_low, _, has_high, _ in peers for there in (has_low, has_high)
    )
    pl.semaphore_wait(barrier, count)


def remote(source, target, sends, receives, index, peer):
    return pltpu.make_async_remote_copy(
        src_ref=source,
        dst_ref=target,
        send_sem=sends.at[index],
        recv_sem=receives.at[index],
        device_id=peer,
        device_id_type=pl.DeviceIdType.MESH,
    )


def gather_kernel(
    axes,
    own_ref,
    measured_ref,
    sort_ref,
    unsort_ref,
    right_ref,
    below_ref,
    corner_ref,
    sorted_ref,
    sent,
    sends,
    receives,
):
    side_len = measured_ref.shape[-1]
    scan, tile = neighbours(axes)
    has_left, left, has_right, _ = scan
    has_up, up, has_down, _ = tile
    sent[:, :side_len, :] = own_ref[:, :side_len, :].astype(jnp.bfloat16)
    sent[:, side_len:, :side_len] = own_ref[:, side_len:, :side_len].astype(jnp.bfloat16)
    meet((scan, tile))
    top = remote(
        sent.at[:, :side_len, :side_len], right_ref.at[:, :side_len, :], sends, receives, 0, left
    )
    rest = remote(
        sent.at[:, side_len:, :side_len], right_ref.at[:, side_len:, :], sends, receives, 1, left
    )
    under = remote(sent.at[:, :side_len, :], below_ref, sends, receives, 2, up)
    corner = remote(right_ref.at[:, :side_len, :], corner_ref, sends, receives, 3, up)

    @pl.when(has_left)
    def _():
        top.start()
        rest.start()

    @pl.when(has_up)
    def _():
        under.start()

    @pl.when(jnp.logical_not(has_right))
    def _():
        right_ref[...] = jnp.zeros_like(right_ref)

    @pl.when(jnp.logical_not(has_down))
    def _():
        below_ref[...] = jnp.zeros_like(below_ref)
        corner_ref[...] = jnp.zeros_like(corner_ref)

    def sort_slot(slot, carry):
        rows = dot(sort_ref[...], measured_ref[slot]).astype(jnp.bfloat16)
        sorted_ref[slot] = dot(rows, unsort_ref[...]).astype(jnp.bfloat16)
        return carry

    lax.fori_loop(0, measured_ref.shape[0], sort_slot, 0)

    @pl.when(has_right)
    def _():
        top.wait_recv()

    @pl.when(has_up)
    def _():
        corner.start()

    @pl.when(has_right)
    def _():
        rest.wait_recv()

    @pl.when(has_down)
    def _():
        under.wait_recv()
        corner.wait_recv()

    @pl.when(has_left)
    def _():
        top.wait_send()
        rest.wait_send()

    @pl.when(has_up)
    def _():
        under.wait_send()
        corner.wait_send()


def gather(axes, own, measured):
    side_len = measured.shape[-1]
    tile_len = own.shape[1]
    vmem = pl.BlockSpec(memory_space=pltpu.VMEM)
    return pl.pallas_call(
        functools.partial(gather_kernel, axes),
        out_shape=[
            jax.ShapeDtypeStruct((2, tile_len, side_len), jnp.bfloat16),
            jax.ShapeDtypeStruct((2, side_len, tile_len), jnp.bfloat16),
            jax.ShapeDtypeStruct((2, side_len, side_len), jnp.bfloat16),
            jax.ShapeDtypeStruct(measured.shape, jnp.bfloat16),
        ],
        in_specs=[vmem] * 4,
        out_specs=[vmem] * 4,
        scratch_shapes=[
            pltpu.VMEM((2, tile_len, tile_len), jnp.bfloat16),
            pltpu.SemaphoreType.DMA((4,)),
            pltpu.SemaphoreType.DMA((4,)),
        ],
        compiler_params=pltpu.CompilerParams(
            collective_id=0, has_side_effects=True, vmem_limit_bytes=40 * 1024 * 1024
        ),
    )(own, measured, *sorted_by_residue(side_len))


def scatter_kernel(
    axes,
    spill_ref,
    drop_ref,
    both_ref,
    from_left_ref,
    from_up_ref,
    joined,
    landed,
    sends,
    receives,
):
    side_len = both_ref.shape[1]
    scan, tile = neighbours(axes)
    has_left, _, has_right, right = scan
    has_up, _, has_down, down = tile
    meet((scan, tile))
    corner = remote(both_ref, landed, sends, receives, 0, down)
    under = remote(drop_ref, from_up_ref, sends, receives, 1, down)
    rest = remote(
        spill_ref.at[:, side_len:, :], from_left_ref.at[:, side_len:, :], sends, receives, 2, right
    )
    top = remote(joined, from_left_ref.at[:, :side_len, :], sends, receives, 3, right)

    @pl.when(has_down)
    def _():
        corner.start()

    @pl.when(has_right)
    def _():
        rest.start()

    @pl.when(has_down)
    def _():
        under.start()

    @pl.when(jnp.logical_not(has_left))
    def _():
        from_left_ref[...] = jnp.zeros_like(from_left_ref)

    @pl.when(jnp.logical_not(has_up))
    def _():
        from_up_ref[...] = jnp.zeros_like(from_up_ref)
        landed[...] = jnp.zeros_like(landed)

    @pl.when(has_up)
    def _():
        corner.wait_recv()

    joined[...] = (
        spill_ref[:, :side_len, :].astype(jnp.float32) + landed[...].astype(jnp.float32)
    ).astype(jnp.bfloat16)

    @pl.when(has_right)
    def _():
        top.start()

    @pl.when(has_left)
    def _():
        rest.wait_recv()
        top.wait_recv()

    @pl.when(has_up)
    def _():
        under.wait_recv()

    @pl.when(has_right)
    def _():
        rest.wait_send()
        top.wait_send()

    @pl.when(has_down)
    def _():
        corner.wait_send()
        under.wait_send()


def scatter(axes, spill, dropped, both):
    vmem = pl.BlockSpec(memory_space=pltpu.VMEM)
    return pl.pallas_call(
        functools.partial(scatter_kernel, axes),
        out_shape=[
            jax.ShapeDtypeStruct(spill.shape, jnp.bfloat16),
            jax.ShapeDtypeStruct(dropped.shape, jnp.bfloat16),
        ],
        in_specs=[vmem] * 3,
        out_specs=[vmem] * 2,
        scratch_shapes=[
            pltpu.VMEM(both.shape, jnp.bfloat16),
            pltpu.VMEM(both.shape, jnp.bfloat16),
            pltpu.SemaphoreType.DMA((4,)),
            pltpu.SemaphoreType.DMA((4,)),
        ],
        compiler_params=pltpu.CompilerParams(
            collective_id=1, has_side_effects=True, vmem_limit_bytes=30 * 1024 * 1024
        ),
    )(spill, dropped, both)


def solve_kernel(
    live_ref,
    shift_ref,
    own_ref,
    right_ref,
    below_ref,
    corner_ref,
    probe_ref,
    measured_ref,
    rows_ref,
    cols_ref,
    out_ref,
    out_right_ref,
    out_below_ref,
    out_corner_ref,
    field,
    grown,
    mixed,
    spectra,
    backs,
):
    tile_len = own_ref.shape[1]
    side_len = probe_ref.shape[1]
    part = side_len // RADIX
    own_blocks = tile_len // LANES
    side_blocks = side_len // LANES
    lane = lax.broadcasted_iota(jnp.int32, (1, LANES), 1)

    for c in range(2):
        for b in range(own_blocks):
            at = slice(b * LANES, (b + 1) * LANES)
            field[c, b, :tile_len, :] = own_ref[c, :, at]
            field[c, b, tile_len:, :] = below_ref[c, :, at].astype(jnp.float32)
        for b in range(side_blocks):
            at = slice(b * LANES, (b + 1) * LANES)
            field[c, own_blocks + b, :tile_len, :] = right_ref[c, :, at].astype(jnp.float32)
            field[c, own_blocks + b, tile_len:, :] = corner_ref[c, :, at].astype(jnp.float32)
    grown[...] = jnp.zeros_like(grown)

    def one_slot(slot, carry):
        row = shift_ref[slot, 0]
        col = shift_ref[slot, 1]
        block = lax.div(col, LANES)
        turn = lax.rem(col, LANES)
        back_turn = lax.rem(LANES - turn, LANES)
        keep = lane < LANES - turn
        enter = lane >= turn
        height = 16

        def load_rows(i, carry):
            at = pl.multiple_of(i * height, height)
            waves = []
            for p in range(RADIX):
                cuts = []
                for c in range(2):
                    turned = [
                        pltpu.roll(
                            field[c, block + b, pl.ds(row + at + p * part, height), :], back_turn, 1
                        )
                        for b in range(side_blocks + 1)
                    ]
                    cuts.append(
                        [jnp.where(keep, turned[b], turned[b + 1]) for b in range(side_blocks)]
                    )
                blocks = []
                for b in range(side_blocks):
                    cols = slice(b * LANES, (b + 1) * LANES)
                    probe_re = probe_ref[0, pl.ds(at + p * part, height), cols]
                    probe_im = probe_ref[1, pl.ds(at + p * part, height), cols]
                    re, im = cuts[0][b], cuts[1][b]
                    blocks.append((probe_re * re - probe_im * im, probe_re * im + probe_im * re))
                waves.append(blocks)
            for b in range(side_blocks):
                cols = slice(b * LANES, (b + 1) * LANES)
                sums = butterfly([waves[p][b] for p in range(RADIX)], -1)
                for q in range(RADIX):
                    mixed[q, pl.ds(at, height), cols] = sums[q][0].astype(jnp.bfloat16)
                    mixed[q, pl.ds(at + part, height), cols] = sums[q][1].astype(jnp.bfloat16)
            return carry

        lax.fori_loop(0, part // height, load_rows, 0)

        for q in range(RADIX):
            half = dot(rows_ref[q], mixed[q])
            parts = [
                (half[:part, p * part : (p + 1) * part], half[part:, p * part : (p + 1) * part])
                for p in range(RADIX)
            ]
            misfits = []
            for other, (re, im) in enumerate(butterfly(parts, -1)):
                far = dot(jnp.concatenate([re, im], axis=1).astype(jnp.bfloat16), cols_ref[other])
                far_re, far_im = far[:, :part], far[:, part:]
                seen = measured_ref[
                    slot, q * part : (q + 1) * part, other * part : (other + 1) * part
                ].astype(jnp.float32)
                misfit = far_re * far_re + far_im * far_im - seen
                misfits.append(
                    jnp.concatenate([misfit * far_re, misfit * far_im], axis=0).astype(jnp.bfloat16)
                )
            spectra[q] = dot(cols_ref[q], jnp.concatenate(misfits, axis=1))

        def mix_rows(i, carry):
            at = pl.multiple_of(i * height, height)
            for other in range(RADIX):
                cols = slice(other * part, (other + 1) * part)
                parts = [
                    (spectra[q, pl.ds(at, height), cols], spectra[q, pl.ds(at + part, height), cols])
                    for q in range(RADIX)
                ]
                for p, (re, im) in enumerate(butterfly(parts, 1)):
                    backs[other, pl.ds(at + p * part, height), :] = jnp.concatenate(
                        [re, im], axis=1
                    ).astype(jnp.bfloat16)
            return carry

        lax.fori_loop(0, part // height, mix_rows, 0)

        def add_rows(i, carry):
            tall = 64
            at = pl.multiple_of(i * tall, tall)
            parts = []
            for other in range(RADIX):
                grad = dot(backs[other, pl.ds(at, tall), :], rows_ref[other])
                parts.append((grad[:, :part], grad[:, part:]))
            turned = [[], []]
            for b, (re, im) in enumerate(butterfly(parts, 1)):
                cols = slice(b * part, (b + 1) * part)
                probe_re = probe_ref[0, pl.ds(at, tall), cols]
                probe_im = probe_ref[1, pl.ds(at, tall), cols]
                turned[0].append(pltpu.roll(probe_re * re + probe_im * im, turn, 1))
                turned[1].append(pltpu.roll(probe_re * im - probe_im * re, turn, 1))
            for c in range(2):
                for b in range(side_blocks + 1):
                    if b == 0:
                        value = jnp.where(enter, turned[c][0], 0.0)
                    elif b == side_blocks:
                        value = jnp.where(enter, 0.0, turned[c][b - 1])
                    else:
                        value = jnp.where(enter, turned[c][b], turned[c][b - 1])
                    grown[c, block + b, pl.ds(row + at, tall), :] += value
            return carry

        lax.fori_loop(0, side_len // 64, add_rows, 0)
        return carry

    lax.fori_loop(0, live_ref[0], one_slot, 0)

    for c in range(2):
        for b in range(own_blocks):
            at = slice(b * LANES, (b + 1) * LANES)
            out_ref[c, :, at] = grown[c, b, :tile_len, :]
            out_below_ref[c, :, at] = grown[c, b, tile_len:, :].astype(jnp.bfloat16)
        for b in range(side_blocks):
            at = slice(b * LANES, (b + 1) * LANES)
            out_right_ref[c, :, at] = grown[c, own_blocks + b, :tile_len, :].astype(jnp.bfloat16)
            out_corner_ref[c, :, at] = grown[c, own_blocks + b, tile_len:, :].astype(jnp.bfloat16)


def solve(live_total, shifts, own, right, below, corner, probe, measured, tables):
    tile_len = own.shape[1]
    side_len = probe.shape[1]
    blocks = (tile_len + side_len) // LANES
    smem = pl.BlockSpec(memory_space=pltpu.SMEM)
    vmem = pl.BlockSpec(memory_space=pltpu.VMEM)
    part = side_len // RADIX
    return pl.pallas_call(
        solve_kernel,
        out_shape=[
            jax.ShapeDtypeStruct(own.shape, jnp.float32),
            jax.ShapeDtypeStruct(right.shape, jnp.bfloat16),
            jax.ShapeDtypeStruct(below.shape, jnp.bfloat16),
            jax.ShapeDtypeStruct(corner.shape, jnp.bfloat16),
        ],
        in_specs=[smem, smem] + [vmem] * 8,
        out_specs=[vmem] * 4,
        scratch_shapes=[
            pltpu.VMEM((2, blocks, tile_len + side_len, LANES), jnp.float32),
            pltpu.VMEM((2, blocks, tile_len + side_len, LANES), jnp.float32),
            pltpu.VMEM((RADIX, 2 * part, side_len), jnp.bfloat16),
            pltpu.VMEM((RADIX, 2 * part, side_len), jnp.float32),
            pltpu.VMEM((RADIX, side_len, 2 * part), jnp.bfloat16),
        ],
        compiler_params=pltpu.CompilerParams(vmem_limit_bytes=60 * 1024 * 1024),
    )(live_total, shifts, own, right, below, corner, probe, measured, *tables)


def add_kernel(own_ref, left_ref, up_ref, out_ref):
    side_len = left_ref.shape[2]
    row_blocks = up_ref.shape[1] // own_ref.shape[1]
    total = own_ref[...]
    out_ref[:, :, :side_len] = total[:, :, :side_len] + left_ref[...].astype(jnp.float32)
    out_ref[:, :, side_len:] = total[:, :, side_len:]

    @pl.when(pl.program_id(0) < row_blocks)
    def _():
        height = own_ref.shape[1]
        at = pl.multiple_of(pl.program_id(0) * height, height)
        out_ref[...] += up_ref[:, pl.ds(at, height), :].astype(jnp.float32)


def add_received(own, from_left, from_up):
    height = LANES
    return pl.pallas_call(
        add_kernel,
        grid=(own.shape[1] // height,),
        out_shape=jax.ShapeDtypeStruct(own.shape, jnp.float32),
        in_specs=[
            pl.BlockSpec((2, height, own.shape[2]), lambda i: (0, i, 0)),
            pl.BlockSpec((2, height, from_left.shape[2]), lambda i: (0, i, 0)),
            pl.BlockSpec(memory_space=pltpu.VMEM),
        ],
        out_specs=pl.BlockSpec((2, height, own.shape[2]), lambda i: (0, i, 0)),
    )(own, from_left, from_up)


def shards(axes, object_slab, probe_field, intensities, offsets, live_count):
    right, below, corner, measured = gather(axes, object_slab, intensities[0, 0])
    live_total = live_count[lax.axis_index("scan")]
    tables = residue_tables(probe_field.shape[-1])
    own, spill, dropped, both = solve(
        live_total, offsets[0, 0], object_slab, right, below, corner, probe_field, measured, tables
    )
    from_left, from_up = scatter(axes, spill, dropped, both)
    return add_received(own, from_left, from_up)


def solution(mesh):
    placed = (
        P(None, "tile", "scan"),
        P(),
        P("scan", "tile", None, None, None),
        P("scan", "tile", None, None),
        P(None, "tile"),
    )
    axes = tuple((name, mesh.shape[name]) for name in ("scan", "tile"))
    return jax.shard_map(
        functools.partial(shards, axes), mesh=mesh, in_specs=placed, out_specs=P(None, "tile", "scan"), check_vma=False
    )
```

profile of v0, /device:TPU:9, one launch (start us, length us, event | category | flops | bytes accessed | tf_op | source)
XLA Modules:
  0.0 152.2 jit_solution(12933238563777670972)
XLA Ops:
  0.0 0.0 copy-start
  0.0 0.7 copy-done
  0.7 0.6 constant_dynamic-slice_fusion
  1.2 1.3 copy.10.shift_ref
  2.6 0.0 copy-start.2
  2.6 1.9 %copy-done.2 = bf16[1,1,6,512,512]{4,3,2,1,0:T(8,128)(2,1)S(1)} copy-done((bf16[1,1,6,512,512]{4,3,2,1,0:T(8,128)(2,1)S(1)}, bf16[1,1,6,512,512]{4,3,2,1,0:T(8,128)(2,1)}, u32[]{:S(2)}) %copy-start.2) | copy-done | bytes 3145752
  4.5 0.0 copy-start.11
  4.5 1.0 copy-done.11
  5.5 0.0 copy-start.12
  5.5 1.0 copy-done.12
  6.5 43.9 %shard_map.91 = (bf16[2,768,512]{2,1,0:T(8,128)(2,1)S(1)}, bf16[2,512,768]{2,1,0:T(8,128)(2,1)S(1)}, bf16[2,512,512]{2,1,0:T(8,128)(2,1)S(1)}, bf16[6,512,512]{2,1,0:T(8,128)(2,1)S(1)}) custom-call(f32[2,768,768]{2,1,0:T(8,128)} %own_ref.3, bf16[6,512,512]{2,1,0:T(8,128)(2,1)S(1)} %bitcast.3, bf16[512,512]{1,0:T(8,128)(2,1)S(1)} %copy-done.12, ...), custom_call_target="tpu_custom_call" | custom-call | tf_op jit(solution)/shard_map/pallas_call | solution.py:174
  50.5 0.0 copy-start.1
  50.5 1.7 %copy-done.1 = bf16[6,512,512]{2,1,0:T(8,128)(2,1)} copy-done((bf16[6,512,512]{2,1,0:T(8,128)(2,1)}, bf16[6,512,512]{2,1,0:T(8,128)(2,1)S(1)}, u32[]{:S(2)}) %copy-start.1) | copy-done | bytes 3145752
  52.2 0.0 copy-start.3
  52.2 1.2 copy-done.3
  53.3 0.0 copy-start.4
  53.3 1.1 copy-done.4
  54.5 0.0 copy-start.9
  54.5 1.0 copy-done.9
  55.5 17.8 %shard_map.92 = (f32[2,768,768]{2,1,0:T(8,128)}, bf16[2,768,512]{2,1,0:T(8,128)(2,1)}, bf16[2,512,768]{2,1,0:T(8,128)(2,1)}, bf16[2,512,512]{2,1,0:T(8,128)(2,1)}) custom-call(s32[1]{0:T(128)} %bitcast.live_ref, s32[6,2]{1,0:T(8,128)} %copy.10.shift_ref, f32[2,768,768]{2,1,0:T(8,128)} %own_ref.3, bf16[2,768,512]{2,1,0:T(8,128)(2,1)} %copy-done.3, ...), custom_call_target="tpu_custom_call" | custom-call | tf_op jit(solution)/shard_map/pallas_call | solution.py:459
  73.3 0.0 copy-start.7
  73.3 1.4 copy-done.7
  74.7 0.0 copy-start.8
  74.7 1.4 copy-done.8
  76.1 0.0 copy-start.10
  76.1 1.2 copy-done.10
  77.3 65.7 %shard_map.93 = (bf16[2,768,512]{2,1,0:T(8,128)(2,1)S(1)}, bf16[2,512,768]{2,1,0:T(8,128)(2,1)S(1)}) custom-call(bf16[2,768,512]{2,1,0:T(8,128)(2,1)S(1)} %copy-done.7, bf16[2,512,768]{2,1,0:T(8,128)(2,1)S(1)} %copy-done.8, bf16[2,512,512]{2,1,0:T(8,128)(2,1)S(1)} %copy-done.10), custom_call_target="tpu_custom_call" | custom-call | tf_op jit(solution)/shard_map/pallas_call | solution.py:274
  143.0 0.0 copy-start.5
  143.0 1.2 copy-done.5
  144.2 0.0 copy-start.6
  144.2 1.1 copy-done.6
  145.3 6.9 %shard_map.94 = f32[2,768,768]{2,1,0:T(8,128)} custom-call(f32[2,768,768]{2,1,0:T(8,128)} %get-tuple-element.19.own_ref, bf16[2,768,512]{2,1,0:T(8,128)(2,1)} %copy-done.5, bf16[2,512,768]{2,1,0:T(8,128)(2,1)} %copy-done.6), custom_call_target="tpu_custom_call" | custom-call | tf_op jit(solution)/shard_map/pallas_call | solution.py:496
Async XLA Ops:
  0.0 0.7 copy-start
  2.6 1.9 %copy-start.2 = (bf16[1,1,6,512,512]{4,3,2,1,0:T(8,128)(2,1)S(1)}, bf16[1,1,6,512,512]{4,3,2,1,0:T(8,128)(2,1)}, u32[]{:S(2)}) copy-start(bf16[1,1,6,512,512]{4,3,2,1,0:T(8,128)(2,1)} %param.11) | copy-start | bytes 9437188
  4.5 1.0 copy-start.11
  5.5 1.0 copy-start.12
  50.5 1.7 %copy-start.1 = (bf16[6,512,512]{2,1,0:T(8,128)(2,1)}, bf16[6,512,512]{2,1,0:T(8,128)(2,1)S(1)}, u32[]{:S(2)}) copy-start(bf16[6,512,512]{2,1,0:T(8,128)(2,1)S(1)} %get-tuple-element.18.measured_ref) | copy-start | bytes 9437188
  52.2 1.2 copy-start.3
  53.3 1.1 copy-start.4
  54.5 1.0 copy-start.9
  73.3 1.4 copy-start.7
  74.7 1.4 copy-start.8
  76.1 1.2 copy-start.10
  143.0 1.2 copy-start.5
  144.2 1.1 copy-start.6
where the time goes:
time: 155 us; the launch traced here: 152 us
  Pallas kernels  134 us (86%)
  local copies, waits for them, and re-layouts  17.9 us (12%)
    pallas_call x1, Pallas kernels, scatter(): pl.pallas_call(functools.partial(scatter_kernel, axes), out_shape=[jax.Sh...  65.7 us
    pallas_call x1, Pallas kernels, gather(): pl.pallas_call(functools.partial(gather_kernel, axes), out_shape=[jax.Sha...  43.9 us
    pallas_call x1, Pallas kernels, solve(): pl.pallas_call(solve_kernel, out_shape=[jax.ShapeDtypeStruct(own.shape, j...  17.8 us
    unnamed x26, local copies, waits for them, and re-layouts  15.9 us
    pallas_call x1, Pallas kernels, add_received(): pl.pallas_call(add_kernel, grid=(own.shape[1] // height,), out_shape=jax....  6.87 us

commit v1 on v0

--- a/solution.py
+++ b/solution.py
@@ -86,37 +86,73 @@
 
 def gather_kernel(
     axes,
-    own_ref,
-    measured_ref,
-    sort_ref,
-    unsort_ref,
-    right_ref,
-    below_ref,
-    corner_ref,
-    sorted_ref,
+    own_hbm,
+    measured_hbm,
+    sort_hbm,
+    unsort_hbm,
+    right_hbm,
+    below_hbm,
+    corner_hbm,
+    sorted_hbm,
+    own,
     sent,
+    right,
+    below,
+    corner,
+    measured,
+    arranged,
+    sort,
+    unsort,
     sends,
     receives,
+    fetches,
+    puts,
 ):
-    side_len = measured_ref.shape[-1]
+    side_len = measured.shape[-1]
     scan, tile = neighbours(axes)
     has_left, left, has_right, _ = scan
     has_up, up, has_down, _ = tile
-    sent[:, :side_len, :] = own_ref[:, :side_len, :].astype(jnp.bfloat16)
-    sent[:, side_len:, :side_len] = own_ref[:, side_len:, :side_len].astype(jnp.bfloat16)
+    first = pltpu.make_async_copy(
+        own_hbm.at[:, :side_len, :side_len], own.at[:, :side_len, :side_len], fetches.at[0]
+    )
+    second = pltpu.make_async_copy(
+        own_hbm.at[:, side_len:, :side_len], own.at[:, side_len:, :side_len], fetches.at[1]
+    )
+    third = pltpu.make_async_copy(
+        own_hbm.at[:, :side_len, side_len:], own.at[:, :side_len, side_len:], fetches.at[2]
+    )
+    fetch_measured = pltpu.make_async_copy(measured_hbm, measured, fetches.at[3])
+    fetch_sort = pltpu.make_async_copy(sort_hbm, sort, fetches.at[4])
+    fetch_unsort = pltpu.make_async_copy(unsort_hbm, unsort, fetches.at[5])
+    first.start()
+    second.start()
+    third.start()
+    fetch_sort.start()
+    fetch_unsort.start()
+    fetch_measured.start()
+    top = remote(
+        sent.at[:, :side_len, :side_len], right.at[:, :side_len, :], sends, receives, 0, left
+    )
+    rest = remote(
+        sent.at[:, side_len:, :side_len], right.at[:, side_len:, :], sends, receives, 1, left
+    )
+    under = remote(sent.at[:, :side_len, :], below, sends, receives, 2, up)
+    across = remote(right.at[:, :side_len, :], corner, sends, receives, 3, up)
+    first.wait()
+    sent[:, :side_len, :side_len] = own[:, :side_len, :side_len].astype(jnp.bfloat16)
     meet((scan, tile))
-    top = remote(
-        sent.at[:, :side_len, :side_len], right_ref.at[:, :side_len, :], sends, receives, 0, left
-    )
-    rest = remote(
-        sent.at[:, side_len:, :side_len], right_ref.at[:, side_len:, :], sends, receives, 1, left
-    )
-    under = remote(sent.at[:, :side_len, :], below_ref, sends, receives, 2, up)
-    corner = remote(right_ref.at[:, :side_len, :], corner_ref, sends, receives, 3, up)
 
     @pl.when(has_left)
     def _():
         top.start()
+
+    second.wait()
+    third.wait()
+    sent[:, side_len:, :side_len] = own[:, side_len:, :side_len].astype(jnp.bfloat16)
+    sent[:, :side_len, side_len:] = own[:, :side_len, side_len:].astype(jnp.bfloat16)
+
+    @pl.when(has_left)
+    def _():
         rest.start()
 
     @pl.when(has_up)
@@ -125,19 +161,25 @@
 
     @pl.when(jnp.logical_not(has_right))
     def _():
-        right_ref[...] = jnp.zeros_like(right_ref)
+        right[...] = jnp.zeros_like(right)
 
     @pl.when(jnp.logical_not(has_down))
     def _():
-        below_ref[...] = jnp.zeros_like(below_ref)
-        corner_ref[...] = jnp.zeros_like(corner_ref)
+        below[...] = jnp.zeros_like(below)
+        corner[...] = jnp.zeros_like(corner)
+
+    fetch_sort.wait()
+    fetch_unsort.wait()
+    fetch_measured.wait()
 
     def sort_slot(slot, carry):
-        rows = dot(sort_ref[...], measured_ref[slot]).astype(jnp.bfloat16)
-        sorted_ref[slot] = dot(rows, unsort_ref[...]).astype(jnp.bfloat16)
+        rows = dot(sort[...], measured[slot]).astype(jnp.bfloat16)
+        arranged[slot] = dot(rows, unsort[...]).astype(jnp.bfloat16)
         return carry
 
-    lax.fori_loop(0, measured_ref.shape[0], sort_slot, 0)
+    lax.fori_loop(0, measured.shape[0], sort_slot, 0)
+    put_sorted = pltpu.make_async_copy(arranged, sorted_hbm, puts.at[0])
+    put_sorted.start()
 
     @pl.when(has_right)
     def _():
@@ -145,16 +187,35 @@
 
     @pl.when(has_up)
     def _():
-        corner.start()
+        across.start()
+
+    put_top = pltpu.make_async_copy(
+        right.at[:, :side_len, :], right_hbm.at[:, :side_len, :], puts.at[1]
+    )
+    put_top.start()
+
+    @pl.when(has_down)
+    def _():
+        under.wait_recv()
+
+    put_below = pltpu.make_async_copy(below, below_hbm, puts.at[2])
+    put_below.start()
 
     @pl.when(has_right)
     def _():
         rest.wait_recv()
 
+    put_rest = pltpu.make_async_copy(
+        right.at[:, side_len:, :], right_hbm.at[:, side_len:, :], puts.at[3]
+    )
+    put_rest.start()
+
     @pl.when(has_down)
     def _():
-        under.wait_recv()
-        corner.wait_recv()
+        across.wait_recv()
+
+    put_corner = pltpu.make_async_copy(corner, corner_hbm, puts.at[4])
+    put_corner.start()
 
     @pl.when(has_left)
     def _():
@@ -164,57 +225,84 @@
     @pl.when(has_up)
     def _():
         under.wait_send()
-        corner.wait_send()
+        across.wait_send()
+
+    put_sorted.wait()
+    put_top.wait()
+    put_below.wait()
+    put_rest.wait()
+    put_corner.wait()
 
 
 def gather(axes, own, measured):
     side_len = measured.shape[-1]
     tile_len = own.shape[1]
-    vmem = pl.BlockSpec(memory_space=pltpu.VMEM)
+    hbm = pl.BlockSpec(memory_space=pltpu.HBM)
+    right = (2, tile_len, side_len)
+    below = (2, side_len, tile_len)
+    corner = (2, side_len, side_len)
     return pl.pallas_call(
         functools.partial(gather_kernel, axes),
         out_shape=[
-            jax.ShapeDtypeStruct((2, tile_len, side_len), jnp.bfloat16),
-            jax.ShapeDtypeStruct((2, side_len, tile_len), jnp.bfloat16),
-            jax.ShapeDtypeStruct((2, side_len, side_len), jnp.bfloat16),
-            jax.ShapeDtypeStruct(measured.shape, jnp.bfloat16),
+            jax.ShapeDtypeStruct(shape, jnp.bfloat16)
+            for shape in (right, below, corner, measured.shape)
         ],
-        in_specs=[vmem] * 4,
-        out_specs=[vmem] * 4,
+        in_specs=[hbm] * 4,
+        out_specs=[hbm] * 4,
         scratch_shapes=[
-            pltpu.VMEM((2, tile_len, tile_len), jnp.bfloat16),
+            pltpu.VMEM(own.shape, jnp.float32),
+            pltpu.VMEM(own.shape, jnp.bfloat16),
+            pltpu.VMEM(right, jnp.bfloat16),
+            pltpu.VMEM(below, jnp.bfloat16),
+            pltpu.VMEM(corner, jnp.bfloat16),
+            pltpu.VMEM(measured.shape, jnp.bfloat16),
+            pltpu.VMEM(measured.shape, jnp.bfloat16),
+            pltpu.VMEM((side_len, side_len), jnp.bfloat16),
+            pltpu.VMEM((side_len, side_len), jnp.bfloat16),
             pltpu.SemaphoreType.DMA((4,)),
             pltpu.SemaphoreType.DMA((4,)),
+            pltpu.SemaphoreType.DMA((6,)),
+            pltpu.SemaphoreType.DMA((5,)),
         ],
         compiler_params=pltpu.CompilerParams(
-            collective_id=0, has_side_effects=True, vmem_limit_bytes=40 * 1024 * 1024
+            collective_id=0, has_side_effects=True, vmem_limit_bytes=48 * 1024 * 1024
         ),
     )(own, measured, *sorted_by_residue(side_len))
 
 
 def scatter_kernel(
     axes,
-    spill_ref,
-    drop_ref,
-    both_ref,
-    from_left_ref,
-    from_up_ref,
+    own_hbm,
+    spill_hbm,
+    drop_hbm,
+    both_hbm,
+    out_hbm,
+    total,
+    spill,
     joined,
     landed,
+    from_left,
+    from_up,
     sends,
     receives,
+    fetches,
+    puts,
 ):
-    side_len = both_ref.shape[1]
+    side_len = landed.shape[1]
     scan, tile = neighbours(axes)
     has_left, _, has_right, right = scan
     has_up, _, has_down, down = tile
+    fetch_spill = pltpu.make_async_copy(spill_hbm.at[:, :side_len, :], spill, fetches.at[0])
+    fetch_own = pltpu.make_async_copy(own_hbm, total, fetches.at[1])
+    fetch_spill.start()
+    fetch_own.start()
     meet((scan, tile))
-    corner = remote(both_ref, landed, sends, receives, 0, down)
-    under = remote(drop_ref, from_up_ref, sends, receives, 1, down)
+    corner = remote(both_hbm, landed, sends, receives, 0, down)
+    under = remote(drop_hbm, from_up, sends, receives, 1, down)
     rest = remote(
-        spill_ref.at[:, side_len:, :], from_left_ref.at[:, side_len:, :], sends, receives, 2, right
-    )
-    top = remote(joined, from_left_ref.at[:, :side_len, :], sends, receives, 3, right)
+        spill_hbm.at[:, side_len:, :], from_left.at[:, side_len:, :], sends, receives, 2, right
+    )
+    top = remote(joined, from_left.at[:, :side_len, :], sends, receives, 3, right)
 
     @pl.when(has_down)
     def _():
@@ -228,35 +316,55 @@
     def _():
         under.start()
 
-    @pl.when(jnp.logical_not(has_left))
-    def _():
-        from_left_ref[...] = jnp.zeros_like(from_left_ref)
-
     @pl.when(jnp.logical_not(has_up))
     def _():
-        from_up_ref[...] = jnp.zeros_like(from_up_ref)
         landed[...] = jnp.zeros_like(landed)
 
+    fetch_spill.wait()
+
     @pl.when(has_up)
     def _():
         corner.wait_recv()
 
-    joined[...] = (
-        spill_ref[:, :side_len, :].astype(jnp.float32) + landed[...].astype(jnp.float32)
-    ).astype(jnp.bfloat16)
+    joined[...] = (spill[...].astype(jnp.float32) + landed[...].astype(jnp.float32)).astype(
+        jnp.bfloat16
+    )
 
     @pl.when(has_right)
     def _():
         top.start()
 
+    fetch_own.wait()
+
     @pl.when(has_left)
     def _():
         rest.wait_recv()
+        total[:, side_len:, :side_len] += from_left[:, side_len:, :].astype(jnp.float32)
+
+    put_rest = pltpu.make_async_copy(
+        total.at[:, side_len:, :], out_hbm.at[:, side_len:, :], puts.at[0]
+    )
+    put_rest.start()
+
+    @pl.when(has_up)
+    def _():
+        under.wait_recv()
+        total[:, :side_len, :] += from_up[...].astype(jnp.float32)
+
+    put_far = pltpu.make_async_copy(
+        total.at[:, :side_len, side_len:], out_hbm.at[:, :side_len, side_len:], puts.at[1]
+    )
+    put_far.start()
+
+    @pl.when(has_left)
+    def _():
         top.wait_recv()
-
-    @pl.when(has_up)
-    def _():
-        under.wait_recv()
+        total[:, :side_len, :side_len] += from_left[:, :side_len, :].astype(jnp.float32)
+
+    put_top = pltpu.make_async_copy(
+        total.at[:, :side_len, :side_len], out_hbm.at[:, :side_len, :side_len], puts.at[2]
+    )
+    put_top.start()
 
     @pl.when(has_right)
     def _():
@@ -268,33 +376,56 @@
         corner.wait_send()
         under.wait_send()
 
-
-def scatter(axes, spill, dropped, both):
-    vmem = pl.BlockSpec(memory_space=pltpu.VMEM)
+    put_rest.wait()
+    put_far.wait()
+    put_top.wait()
+
+
+def scatter(axes, own, spill, dropped, both):
+    hbm = pl.BlockSpec(memory_space=pltpu.HBM)
     return pl.pallas_call(
         functools.partial(scatter_kernel, axes),
-        out_shape=[
-            jax.ShapeDtypeStruct(spill.shape, jnp.bfloat16),
-            jax.ShapeDtypeStruct(dropped.shape, jnp.bfloat16),
-        ],
-        in_specs=[vmem] * 3,
-        out_specs=[vmem] * 2,
+        out_shape=jax.ShapeDtypeStruct(own.shape, jnp.float32),
+        in_specs=[hbm] * 4,
+        out_specs=hbm,
         scratch_shapes=[
+            pltpu.VMEM(own.shape, jnp.float32),
             pltpu.VMEM(both.shape, jnp.bfloat16),
             pltpu.VMEM(both.shape, jnp.bfloat16),
+            pltpu.VMEM(both.shape, jnp.bfloat16),
+            pltpu.VMEM(spill.shape, jnp.bfloat16),
+            pltpu.VMEM(dropped.shape, jnp.bfloat16),
             pltpu.SemaphoreType.DMA((4,)),
             pltpu.SemaphoreType.DMA((4,)),
+            pltpu.SemaphoreType.DMA((2,)),
+            pltpu.SemaphoreType.DMA((3,)),
         ],
         compiler_params=pltpu.CompilerParams(
-            collective_id=1, has_side_effects=True, vmem_limit_bytes=30 * 1024 * 1024
+            collective_id=1, has_side_effects=True, vmem_limit_bytes=40 * 1024 * 1024
         ),
-    )(spill, dropped, both)
+    )(own, spill, dropped, both)
 
 
 def solve_kernel(
     live_ref,
     shift_ref,
-    own_ref,
+    own_hbm,
+    right_hbm,
+    below_hbm,
+    corner_hbm,
+    probe_hbm,
+    measured_hbm,
+    rows_hbm,
+    cols_hbm,
+    out_hbm,
+    out_right_hbm,
+    out_below_hbm,
+    out_corner_hbm,
+    field,
+    grown,
+    mixed,
+    spectra,
+    backs,
     right_ref,
     below_ref,
     corner_ref,
@@ -302,33 +433,58 @@
     measured_ref,
     rows_ref,
     cols_ref,
-    out_ref,
-    out_right_ref,
-    out_below_ref,
-    out_corner_ref,
-    field,
-    grown,
-    mixed,
-    spectra,
-    backs,
+    fetches,
+    puts,
 ):
-    tile_len = own_ref.shape[1]
+    tile_len = own_hbm.shape[1]
     side_len = probe_ref.shape[1]
     part = side_len // RADIX
     own_blocks = tile_len // LANES
     side_blocks = side_len // LANES
     lane = lax.broadcasted_iota(jnp.int32, (1, LANES), 1)
 
+    loads = [
+        pltpu.make_async_copy(source, target, fetches.at[i])
+        for i, (source, target) in enumerate(
+            (
+                (below_hbm, below_ref),
+                (right_hbm, right_ref),
+                (corner_hbm, corner_ref),
+                (probe_hbm, probe_ref),
+                (rows_hbm, rows_ref),
+                (cols_hbm, cols_ref),
+                (measured_hbm, measured_ref),
+            )
+        )
+    ]
+    for load in loads[:3]:
+        load.start()
+    pieces = [
+        pltpu.make_async_copy(
+            own_hbm.at[c, :, b * LANES : (b + 1) * LANES],
+            field.at[c, b, :tile_len, :],
+            fetches.at[len(loads) + c * own_blocks + b],
+        )
+        for c in range(2)
+        for b in range(own_blocks)
+    ]
+    for load in pieces + loads[3:]:
+        load.start()
+    grown[...] = jnp.zeros_like(grown)
+    loads[0].wait()
     for c in range(2):
         for b in range(own_blocks):
             at = slice(b * LANES, (b + 1) * LANES)
-            field[c, b, :tile_len, :] = own_ref[c, :, at]
             field[c, b, tile_len:, :] = below_ref[c, :, at].astype(jnp.float32)
+    loads[1].wait()
+    loads[2].wait()
+    for c in range(2):
         for b in range(side_blocks):
             at = slice(b * LANES, (b + 1) * LANES)
             field[c, own_blocks + b, :tile_len, :] = right_ref[c, :, at].astype(jnp.float32)
             field[c, own_blocks + b, tile_len:, :] = corner_ref[c, :, at].astype(jnp.float32)
-    grown[...] = jnp.zeros_like(grown)
+    for load in pieces + loads[3:]:
+        load.wait()
 
     def one_slot(slot, carry):
         row = shift_ref[slot, 0]
@@ -371,7 +527,7 @@
                     mixed[q, pl.ds(at + part, height), cols] = sums[q][1].astype(jnp.bfloat16)
             return carry
 
-        lax.fori_loop(0, part // height, load_rows, 0)
+        lax.fori_loop(0, part // height, load_rows, 0, unroll=part // height)
 
         for q in range(RADIX):
             half = dot(rows_ref[q], mixed[q])
@@ -406,10 +562,10 @@
                     ).astype(jnp.bfloat16)
             return carry
 
-        lax.fori_loop(0, part // height, mix_rows, 0)
+        lax.fori_loop(0, part // height, mix_rows, 0, unroll=part // height)
 
         def add_rows(i, carry):
-            tall = 64
+            tall = 256
             at = pl.multiple_of(i * tall, tall)
             parts = []
             for other in range(RADIX):
@@ -433,20 +589,39 @@
                     grown[c, block + b, pl.ds(row + at, tall), :] += value
             return carry
 
-        lax.fori_loop(0, side_len // 64, add_rows, 0)
+        lax.fori_loop(0, side_len // 256, add_rows, 0)
         return carry
 
     lax.fori_loop(0, live_ref[0], one_slot, 0)
 
+    stores = [
+        pltpu.make_async_copy(
+            grown.at[c, b, :tile_len, :],
+            out_hbm.at[c, :, b * LANES : (b + 1) * LANES],
+            puts.at[3 + c * own_blocks + b],
+        )
+        for c in range(2)
+        for b in range(own_blocks)
+    ]
+    for store in stores:
+        store.start()
+    for c in range(2):
+        for b in range(side_blocks):
+            at = slice(b * LANES, (b + 1) * LANES)
+            corner_ref[c, :, at] = grown[c, own_blocks + b, tile_len:, :].astype(jnp.bfloat16)
+            right_ref[c, :, at] = grown[c, own_blocks + b, :tile_len, :].astype(jnp.bfloat16)
+    stores.append(pltpu.make_async_copy(corner_ref, out_corner_hbm, puts.at[0]))
+    stores.append(pltpu.make_async_copy(right_ref, out_right_hbm, puts.at[1]))
+    stores[-2].start()
+    stores[-1].start()
     for c in range(2):
         for b in range(own_blocks):
             at = slice(b * LANES, (b + 1) * LANES)
-            out_ref[c, :, at] = grown[c, b, :tile_len, :]
-            out_below_ref[c, :, at] = grown[c, b, tile_len:, :].astype(jnp.bfloat16)
-        for b in range(side_blocks):
-            at = slice(b * LANES, (b + 1) * LANES)
-            out_right_ref[c, :, at] = grown[c, own_blocks + b, :tile_len, :].astype(jnp.bfloat16)
-            out_corner_ref[c, :, at] = grown[c, own_blocks + b, tile_len:, :].astype(jnp.bfloat16)
+            below_ref[c, :, at] = grown[c, b, tile_len:, :].astype(jnp.bfloat16)
+    stores.append(pltpu.make_async_copy(below_ref, out_below_hbm, puts.at[2]))
+    stores[-1].start()
+    for store in stores:
+        store.wait()
 
 
 def solve(live_total, shifts, own, right, below, corner, probe, measured, tables):
@@ -454,8 +629,9 @@
     side_len = probe.shape[1]
     blocks = (tile_len + side_len) // LANES
     smem = pl.BlockSpec(memory_space=pltpu.SMEM)
-    vmem = pl.BlockSpec(memory_space=pltpu.VMEM)
+    hbm = pl.BlockSpec(memory_space=pltpu.HBM)
     part = side_len // RADIX
+    copies = 2 * (tile_len // LANES)
     return pl.pallas_call(
         solve_kernel,
         out_shape=[
@@ -464,46 +640,26 @@
             jax.ShapeDtypeStruct(below.shape, jnp.bfloat16),
             jax.ShapeDtypeStruct(corner.shape, jnp.bfloat16),
         ],
-        in_specs=[smem, smem] + [vmem] * 8,
-        out_specs=[vmem] * 4,
+        in_specs=[smem, smem] + [hbm] * 8,
+        out_specs=[hbm] * 4,
         scratch_shapes=[
             pltpu.VMEM((2, blocks, tile_len + side_len, LANES), jnp.float32),
             pltpu.VMEM((2, blocks, tile_len + side_len, LANES), jnp.float32),
             pltpu.VMEM((RADIX, 2 * part, side_len), jnp.bfloat16),
             pltpu.VMEM((RADIX, 2 * part, side_len), jnp.float32),
             pltpu.VMEM((RADIX, side_len, 2 * part), jnp.bfloat16),
+            pltpu.VMEM(right.shape, jnp.bfloat16),
+            pltpu.VMEM(below.shape, jnp.bfloat16),
+            pltpu.VMEM(corner.shape, jnp.bfloat16),
+            pltpu.VMEM(probe.shape, jnp.float32),
+            pltpu.VMEM(measured.shape, jnp.bfloat16),
+            pltpu.VMEM(tables[0].shape, jnp.bfloat16),
+            pltpu.VMEM(tables[1].shape, jnp.bfloat16),
+            pltpu.SemaphoreType.DMA((7 + copies,)),
+            pltpu.SemaphoreType.DMA((3 + copies,)),
         ],
         compiler_params=pltpu.CompilerParams(vmem_limit_bytes=60 * 1024 * 1024),
     )(live_total, shifts, own, right, below, corner, probe, measured, *tables)
-
-
-def add_kernel(own_ref, left_ref, up_ref, out_ref):
-    side_len = left_ref.shape[2]
-    row_blocks = up_ref.shape[1] // own_ref.shape[1]
-    total = own_ref[...]
-    out_ref[:, :, :side_len] = total[:, :, :side_len] + left_ref[...].astype(jnp.float32)
-    out_ref[:, :, side_len:] = total[:, :, side_len:]
-
-    @pl.when(pl.program_id(0) < row_blocks)
-    def _():
-        height = own_ref.shape[1]
-        at = pl.multiple_of(pl.program_id(0) * height, height)
-        out_ref[...] += up_ref[:, pl.ds(at, height), :].astype(jnp.float32)
-
-
-def add_received(own, from_left, from_up):
-    height = LANES
-    return pl.pallas_call(
-        add_kernel,
-        grid=(own.shape[1] // height,),
-        out_shape=jax.ShapeDtypeStruct(own.shape, jnp.float32),
-        in_specs=[
-            pl.BlockSpec((2, height, own.shape[2]), lambda i: (0, i, 0)),
-            pl.BlockSpec((2, height, from_left.shape[2]), lambda i: (0, i, 0)),
-            pl.BlockSpec(memory_space=pltpu.VMEM),
-        ],
-        out_specs=pl.BlockSpec((2, height, own.shape[2]), lambda i: (0, i, 0)),
-    )(own, from_left, from_up)
 
 
 def shards(axes, object_slab, probe_field, intensities, offsets, live_count):
@@ -513,8 +669,7 @@
     own, spill, dropped, both = solve(
         live_total, offsets[0, 0], object_slab, right, below, corner, probe_field, measured, tables
     )
-    from_left, from_up = scatter(axes, spill, dropped, both)
-    return add_received(own, from_left, from_up)
+    return scatter(axes, own, spill, dropped, both)
 
 
 def solution(mesh):

time: 155 us -> 134 us (0.86); the launches traced: 152 us -> 134 us
  Pallas kernels: 134 us -> 117 us
    pallas_call x2 -> x1, Pallas kernels: 72.5 us -> 58.5 us  [scatter(): pl.pallas_call(functools.partial(scatter_kernel, axes), out_shape=jax.Sha...]
    pallas_call x1, Pallas kernels: 17.8 us -> 15.2 us  [solve(): pl.pallas_call(solve_kernel, out_shape=[jax.ShapeDtypeStruct(own.shape, j...]
    unnamed x26 -> x21, local copies, waits for them, and re-layouts: 15.9 us -> 14.6 us
where the time goes in v1:
time: 134 us
  Pallas kernels  117 us (87%)
  local copies, waits for them, and re-layouts  16.5 us (12%)
    pallas_call x1, Pallas kernels, scatter(): pl.pallas_call(functools.partial(scatter_kernel, axes), out_shape=jax.Sha...  58.5 us
    pallas_call x1, Pallas kernels, gather(): pl.pallas_call(functools.partial(gather_kernel, axes), out_shape=[jax.Sha...  43.3 us
    pallas_call x1, Pallas kernels, solve(): pl.pallas_call(solve_kernel, out_shape=[jax.ShapeDtypeStruct(own.shape, j...  15.2 us
    unnamed x21, local copies, waits for them, and re-layouts  14.6 us

profile of v1, /device:TPU:9, one launch (start us, length us, event | category | flops | bytes accessed | tf_op | source)
XLA Modules:
  0.0 133.5 jit_solution(6131229974225867109)
XLA Ops:
  0.0 0.0 copy-start
  0.0 0.7 copy-done
  0.7 0.6 constant_dynamic-slice_fusion
  1.3 1.4 %copy.10.shift_ref = s32[6,2]{1,0:T(8,128)} copy(s32[6,2]{0,1:T(2,128)} %bitcast.4) | data formatting | bytes 96 | tf_op jit(solution)/shard_map/squeeze | solution.py:670
  2.7 0.0 copy-start.8
  2.7 1.0 copy-done.8
  3.7 0.0 copy-start.9
  3.7 1.0 copy-done.9
  4.7 43.3 %shard_map.91 = (bf16[2,768,512]{2,1,0:T(8,128)(2,1)S(1)}, bf16[2,512,768]{2,1,0:T(8,128)(2,1)S(1)}, bf16[2,512,512]{2,1,0:T(8,128)(2,1)S(1)}, bf16[6,512,512]{2,1,0:T(8,128)(2,1)}) custom-call(f32[2,768,768]{2,1,0:T(8,128)} %own_hbm.3, bf16[6,512,512]{2,1,0:T(8,128)(2,1)} %bitcast.3, bf16[512,512]{1,0:T(8,128)(2,1)S(1)} %copy-done.9, ...), custom_call_target="tpu_custom_call" | custom-call | tf_op jit(solution)/shard_map/pallas_call | solution.py:244
  48.0 0.0 copy-start.2
  48.0 1.1 copy-done.2
  49.2 0.0 copy-start.3
  49.2 1.2 copy-done.3
  50.3 0.0 copy-start.6
  50.3 0.9 copy-done.6
  51.3 15.2 %shard_map.92 = (f32[2,768,768]{2,1,0:T(8,128)}, bf16[2,768,512]{2,1,0:T(8,128)(2,1)}, bf16[2,512,768]{2,1,0:T(8,128)(2,1)}, bf16[2,512,512]{2,1,0:T(8,128)(2,1)}) custom-call(s32[1]{0:T(128)} %bitcast.live_ref, s32[6,2]{1,0:T(8,128)} %copy.10.shift_ref, f32[2,768,768]{2,1,0:T(8,128)} %own_hbm.3, bf16[2,768,512]{2,1,0:T(8,128)(2,1)} %copy-done.2, ...), custom_call_target="tpu_custom_call" | custom-call | tf_op jit(solution)/shard_map/pallas_call | solution.py:635
  66.5 0.0 copy-start.1
  66.5 2.3 %copy-done.1 = f32[2,768,768]{2,1,0:T(8,128)S(1)} copy-done((f32[2,768,768]{2,1,0:T(8,128)S(1)}, f32[2,768,768]{2,1,0:T(8,128)}, u32[]{:S(2)}) %copy-start.1) | copy-done | bytes 4718616
  68.8 0.0 copy-start.4
  68.8 1.4 %copy-done.4 = bf16[2,768,512]{2,1,0:T(8,128)(2,1)S(1)} copy-done((bf16[2,768,512]{2,1,0:T(8,128)(2,1)S(1)}, bf16[2,768,512]{2,1,0:T(8,128)(2,1)}, u32[]{:S(2)}) %copy-start.4) | copy-done | bytes 1572888
  70.2 0.0 copy-start.5
  70.2 1.4 %copy-done.5 = bf16[2,512,768]{2,1,0:T(8,128)(2,1)S(1)} copy-done((bf16[2,512,768]{2,1,0:T(8,128)(2,1)S(1)}, bf16[2,512,768]{2,1,0:T(8,128)(2,1)}, u32[]{:S(2)}) %copy-start.5) | copy-done | bytes 1572888
  71.6 0.0 copy-start.7
  71.6 1.2 copy-done.7
  72.9 58.5 %shard_map.93 = f32[2,768,768]{2,1,0:T(8,128)S(1)} custom-call(f32[2,768,768]{2,1,0:T(8,128)S(1)} %copy-done.1, bf16[2,768,512]{2,1,0:T(8,128)(2,1)S(1)} %copy-done.4, bf16[2,512,768]{2,1,0:T(8,128)(2,1)S(1)} %copy-done.5, bf16[2,512,512]{2,1,0:T(8,128)(2,1)S(1)} %copy-done.7), custom_call_target="tpu_custom_call" | custom-call | tf_op jit(solution)/shard_map/pallas_call | solution.py:386
  131.3 2.2 %copy.12 = f32[2,768,768]{2,1,0:T(8,128)} copy(f32[2,768,768]{2,1,0:T(8,128)S(1)} %shard_map.93) | data formatting | bytes 9437184
Async XLA Ops:
  0.0 0.7 copy-start
  2.7 1.0 copy-start.8
  3.7 1.0 copy-start.9
  48.0 1.1 copy-start.2
  49.2 1.2 copy-start.3
  50.3 0.9 copy-start.6
  66.5 2.3 %copy-start.1 = (f32[2,768,768]{2,1,0:T(8,128)S(1)}, f32[2,768,768]{2,1,0:T(8,128)}, u32[]{:S(2)}) copy-start(f32[2,768,768]{2,1,0:T(8,128)} %get-tuple-element.17.own_hbm) | copy-start | bytes 14155780
  68.8 1.4 %copy-start.4 = (bf16[2,768,512]{2,1,0:T(8,128)(2,1)S(1)}, bf16[2,768,512]{2,1,0:T(8,128)(2,1)}, u32[]{:S(2)}) copy-start(bf16[2,768,512]{2,1,0:T(8,128)(2,1)} %get-tuple-element.18.spill_hbm) | copy-start | bytes 4718596
  70.2 1.4 %copy-start.5 = (bf16[2,512,768]{2,1,0:T(8,128)(2,1)S(1)}, bf16[2,512,768]{2,1,0:T(8,128)(2,1)}, u32[]{:S(2)}) copy-start(bf16[2,512,768]{2,1,0:T(8,128)(2,1)} %get-tuple-element.19.drop_hbm) | copy-start | bytes 4718596
  71.6 1.2 copy-start.7

commit v2 on v1

--- a/solution.py
+++ b/solution.py
@@ -11,6 +11,7 @@
 
 RADIX = 4
 LANES = 128
+vmem_bytes = 67043328
 
 
 def residue_tables(side_len):
@@ -265,7 +266,7 @@
             pltpu.SemaphoreType.DMA((5,)),
         ],
         compiler_params=pltpu.CompilerParams(
-            collective_id=0, has_side_effects=True, vmem_limit_bytes=48 * 1024 * 1024
+            collective_id=0, has_side_effects=True, vmem_limit_bytes=vmem_bytes
         ),
     )(own, measured, *sorted_by_residue(side_len))
 
@@ -401,7 +402,7 @@
             pltpu.SemaphoreType.DMA((3,)),
         ],
         compiler_params=pltpu.CompilerParams(
-            collective_id=1, has_side_effects=True, vmem_limit_bytes=40 * 1024 * 1024
+            collective_id=1, has_side_effects=True, vmem_limit_bytes=vmem_bytes
         ),
     )(own, spill, dropped, both)
 
@@ -487,8 +488,8 @@
         load.wait()
 
     def one_slot(slot, carry):
-        row = shift_ref[slot, 0]
-        col = shift_ref[slot, 1]
+        row = shift_ref[0, slot]
+        col = shift_ref[1, slot]
         block = lax.div(col, LANES)
         turn = lax.rem(col, LANES)
         back_turn = lax.rem(LANES - turn, LANES)
@@ -592,7 +593,7 @@
         lax.fori_loop(0, side_len // 256, add_rows, 0)
         return carry
 
-    lax.fori_loop(0, live_ref[0], one_slot, 0)
+    lax.fori_loop(0, live_ref[0, lax.axis_index("scan")], one_slot, 0)
 
     stores = [
         pltpu.make_async_copy(
@@ -624,7 +625,7 @@
         store.wait()
 
 
-def solve(live_total, shifts, own, right, below, corner, probe, measured, tables):
+def solve(live_counts, shifts, own, right, below, corner, probe, measured, tables):
     tile_len = own.shape[1]
     side_len = probe.shape[1]
     blocks = (tile_len + side_len) // LANES
@@ -658,16 +659,15 @@
             pltpu.SemaphoreType.DMA((7 + copies,)),
             pltpu.SemaphoreType.DMA((3 + copies,)),
         ],
-        compiler_params=pltpu.CompilerParams(vmem_limit_bytes=60 * 1024 * 1024),
-    )(live_total, shifts, own, right, below, corner, probe, measured, *tables)
+        compiler_params=pltpu.CompilerParams(vmem_limit_bytes=vmem_bytes),
+    )(live_counts, shifts, own, right, below, corner, probe, measured, *tables)
 
 
 def shards(axes, object_slab, probe_field, intensities, offsets, live_count):
     right, below, corner, measured = gather(axes, object_slab, intensities[0, 0])
-    live_total = live_count[lax.axis_index("scan")]
     tables = residue_tables(probe_field.shape[-1])
     own, spill, dropped, both = solve(
-        live_total, offsets[0, 0], object_slab, right, below, corner, probe_field, measured, tables
+        live_count.T, offsets[0, 0].T, object_slab, right, below, corner, probe_field, measured, tables
     )
     return scatter(axes, own, spill, dropped, both)
 

time: 134 us -> 124 us (0.925)
  the two profiles are of different devices: /device:TPU:9 before, /device:TPU:17 now
where the time goes in v2:
time: 124 us; the launch traced here: 123 us
  Pallas kernels  118 us (95%)
  local copies, waits for them, and re-layouts  4.83 us (4%)
    pallas_call x1, Pallas kernels, scatter(): pl.pallas_call(functools.partial(scatter_kernel, axes), out_shape=jax.Sha...  59.6 us
    pallas_call x1, Pallas kernels, gather(): pl.pallas_call(functools.partial(gather_kernel, axes), out_shape=[jax.Sha...  44.2 us
    pallas_call x1, Pallas kernels, solve(): pl.pallas_call(solve_kernel, out_shape=[jax.ShapeDtypeStruct(own.shape, j...  14.4 us
    unnamed x1, local copies, waits for them, and re-layouts  4.83 us

profile of v2, /device:TPU:17, one launch (start us, length us, event | category | flops | bytes accessed | tf_op | source)
XLA Modules:
  0.0 123.0 jit_solution(12657783462432334976)
XLA Ops:
  0.0 44.2 %shard_map.91 = (bf16[2,768,512]{2,1,0:T(8,128)(2,1)}, bf16[2,512,768]{2,1,0:T(8,128)(2,1)}, bf16[2,512,512]{2,1,0:T(8,128)(2,1)}, bf16[6,512,512]{2,1,0:T(8,128)(2,1)}) custom-call(f32[2,768,768]{2,1,0:T(8,128)} %own_hbm.3, bf16[6,512,512]{2,1,0:T(8,128)(2,1)} %bitcast.5, bf16[512,512]{1,0:T(8,128)(2,1)} %constant.8.clone.sort_hbm, ...), custom_call_target="tpu_custom_call" | custom-call | tf_op jit(solution)/shard_map/pallas_call | solution.py:245
  44.2 14.4 %shard_map.92 = (f32[2,768,768]{2,1,0:T(8,128)}, bf16[2,768,512]{2,1,0:T(8,128)(2,1)}, bf16[2,512,768]{2,1,0:T(8,128)(2,1)}, bf16[2,512,512]{2,1,0:T(8,128)(2,1)}) custom-call(s32[1,8]{1,0:T(1,128)} %bitcast.7, s32[2,6]{1,0:T(2,128)} %bitcast.6, f32[2,768,768]{2,1,0:T(8,128)} %own_hbm.3, bf16[2,768,512]{2,1,0:T(8,128)(2,1)} %get-tuple-element.13.right_hbm, ...), custom_call_target="tpu_custom_call" | custom-call | tf_op jit(solution)/shard_map/pallas_call | solution.py:636
  58.6 59.6 %shard_map.93 = f32[2,768,768]{2,1,0:T(8,128)} custom-call(f32[2,768,768]{2,1,0:T(8,128)} %get-tuple-element.17.own_hbm, bf16[2,768,512]{2,1,0:T(8,128)(2,1)} %get-tuple-element.18.spill_hbm, bf16[2,512,768]{2,1,0:T(8,128)(2,1)} %get-tuple-element.19.drop_hbm, bf16[2,512,512]{2,1,0:T(8,128)(2,1)} %get-tuple-element.20.both_hbm), custom_call_target="tpu_custom_call" | custom-call | tf_op jit(solution)/shard_map/pallas_call | solution.py:387
  118.2 4.8 %copy.11 = f32[2,768,768]{2,1,0:T(8,128)} copy(f32[2,768,768]{2,1,0:T(8,128)} %shard_map.93) | data formatting | bytes 9437184

commit v3 on v2

--- a/solution.py
+++ b/solution.py
@@ -277,7 +277,6 @@
     spill_hbm,
     drop_hbm,
     both_hbm,
-    out_hbm,
     total,
     spill,
     joined,
@@ -287,7 +286,6 @@
     sends,
     receives,
     fetches,
-    puts,
 ):
     side_len = landed.shape[1]
     scan, tile = neighbours(axes)
@@ -342,31 +340,16 @@
         rest.wait_recv()
         total[:, side_len:, :side_len] += from_left[:, side_len:, :].astype(jnp.float32)
 
-    put_rest = pltpu.make_async_copy(
-        total.at[:, side_len:, :], out_hbm.at[:, side_len:, :], puts.at[0]
-    )
-    put_rest.start()
-
     @pl.when(has_up)
     def _():
         under.wait_recv()
         total[:, :side_len, :] += from_up[...].astype(jnp.float32)
 
-    put_far = pltpu.make_async_copy(
-        total.at[:, :side_len, side_len:], out_hbm.at[:, :side_len, side_len:], puts.at[1]
-    )
-    put_far.start()
-
     @pl.when(has_left)
     def _():
         top.wait_recv()
         total[:, :side_len, :side_len] += from_left[:, :side_len, :].astype(jnp.float32)
 
-    put_top = pltpu.make_async_copy(
-        total.at[:, :side_len, :side_len], out_hbm.at[:, :side_len, :side_len], puts.at[2]
-    )
-    put_top.start()
-
     @pl.when(has_right)
     def _():
         rest.wait_send()
@@ -376,21 +359,16 @@
     def _():
         corner.wait_send()
         under.wait_send()
-
-    put_rest.wait()
-    put_far.wait()
-    put_top.wait()
 
 
 def scatter(axes, own, spill, dropped, both):
     hbm = pl.BlockSpec(memory_space=pltpu.HBM)
     return pl.pallas_call(
         functools.partial(scatter_kernel, axes),
-        out_shape=jax.ShapeDtypeStruct(own.shape, jnp.float32),
+        out_shape=pltpu.VMEM(own.shape, jnp.float32),
         in_specs=[hbm] * 4,
-        out_specs=hbm,
+        out_specs=pl.BlockSpec(memory_space=pltpu.VMEM),
         scratch_shapes=[
-            pltpu.VMEM(own.shape, jnp.float32),
             pltpu.VMEM(both.shape, jnp.bfloat16),
             pltpu.VMEM(both.shape, jnp.bfloat16),
             pltpu.VMEM(both.shape, jnp.bfloat16),
@@ -399,10 +377,9 @@
             pltpu.SemaphoreType.DMA((4,)),
             pltpu.SemaphoreType.DMA((4,)),
             pltpu.SemaphoreType.DMA((2,)),
-            pltpu.SemaphoreType.DMA((3,)),
         ],
         compiler_params=pltpu.CompilerParams(
-            collective_id=1, has_side_effects=True, vmem_limit_bytes=vmem_bytes
+            collective_id=1, has_side_effects=True, vmem_limit_bytes=vmem_bytes - own.size * 4 - (1 << 20)
         ),
     )(own, spill, dropped, both)
 

time: 124 us -> 119 us (0.960)
  the two profiles are of different devices: /device:TPU:17 before, /device:TPU:9 now
where the time goes in v3:
time: 119 us
  Pallas kernels  117 us (98%)
  local copies, waits for them, and re-layouts  2.19 us (2%)
    pallas_call x1, Pallas kernels, scatter(): pl.pallas_call(functools.partial(scatter_kernel, axes), out_shape=pltpu.V...  58.1 us
    pallas_call x1, Pallas kernels, gather(): pl.pallas_call(functools.partial(gather_kernel, axes), out_shape=[jax.Sha...  44.2 us
    pallas_call x1, Pallas kernels, solve(): pl.pallas_call(solve_kernel, out_shape=[jax.ShapeDtypeStruct(own.shape, j...  14.5 us

profile of v3, /device:TPU:9, one launch (start us, length us, event | category | flops | bytes accessed | tf_op | source)
XLA Modules:
  0.0 119.0 jit_solution(11854167041442394072)
XLA Ops:
  0.0 44.2 %shard_map.91 = (bf16[2,768,512]{2,1,0:T(8,128)(2,1)}, bf16[2,512,768]{2,1,0:T(8,128)(2,1)}, bf16[2,512,512]{2,1,0:T(8,128)(2,1)}, bf16[6,512,512]{2,1,0:T(8,128)(2,1)}) custom-call(f32[2,768,768]{2,1,0:T(8,128)} %own_hbm.3, bf16[6,512,512]{2,1,0:T(8,128)(2,1)} %bitcast.5, bf16[512,512]{1,0:T(8,128)(2,1)} %constant.8.clone.sort_hbm, ...), custom_call_target="tpu_custom_call" | custom-call | tf_op jit(solution)/shard_map/pallas_call | solution.py:245
  44.2 14.5 %shard_map.92 = (f32[2,768,768]{2,1,0:T(8,128)}, bf16[2,768,512]{2,1,0:T(8,128)(2,1)}, bf16[2,512,768]{2,1,0:T(8,128)(2,1)}, bf16[2,512,512]{2,1,0:T(8,128)(2,1)}) custom-call(s32[1,8]{1,0:T(1,128)} %bitcast.7, s32[2,6]{1,0:T(2,128)} %bitcast.6, f32[2,768,768]{2,1,0:T(8,128)} %own_hbm.3, bf16[2,768,512]{2,1,0:T(8,128)(2,1)} %get-tuple-element.13.right_hbm, ...), custom_call_target="tpu_custom_call" | custom-call | tf_op jit(solution)/shard_map/pallas_call | solution.py:613
  58.6 58.1 %shard_map.93 = f32[2,768,768]{2,1,0:T(8,128)S(1)} custom-call(f32[2,768,768]{2,1,0:T(8,128)} %get-tuple-element.17.own_hbm, bf16[2,768,512]{2,1,0:T(8,128)(2,1)} %get-tuple-element.18.spill_hbm, bf16[2,512,768]{2,1,0:T(8,128)(2,1)} %get-tuple-element.19.drop_hbm, bf16[2,512,512]{2,1,0:T(8,128)(2,1)} %get-tuple-element.20.both_hbm), custom_call_target="tpu_custom_call" | custom-call | tf_op jit(solution)/shard_map/pallas_call | solution.py:366
  116.8 2.2 %copy.11 = f32[2,768,768]{2,1,0:T(8,128)} copy(f32[2,768,768]{2,1,0:T(8,128)S(1)} %shard_map.93) | data formatting | bytes 9437184
